TPU v7x, 32 devices: a whole 2x2x4 slice. The times are simulated.
32 devices in a mesh: tile: 8 (over z, x), mem: 4 (over y, core).
Axes of the slice: x: 2, y: 2, z: 4, core: 2. Of those that a mesh axis runs over, the one named last changes fastest.
Arguments:
- prior_ensemble_fields: float32 [128, 32, 512], P('mem', 'tile'), may hold values from -6 to 6
- vel_y: float32 [32, 512], P('tile'), may hold values from -0.4 to 0.4
- vel_x: float32 [32, 512], P('tile'), may hold values from -0.4 to 0.4
- diffus: float32 [32, 512], P('tile'), may hold values from 0.02 to 0.2
- assign: int32 [8, 2048], P('tile'), may hold values from 0 to 2047, each once within a row
- obs_cell: int32 [64, 512], P(('tile', 'mem')), may hold values from 0 to 255
- obs_value: float32 [64, 512], P(('tile', 'mem')), may hold values from -6 to 6
- obs_var: float32 [64, 512], P(('tile', 'mem')), may hold values from 0.2 to 2
Outputs:
- analysis: float32 [128, 32, 512], P('mem', 'tile')
All inputs are finite; a program needn't handle non-finite values.
Results may differ from a plain program's by a relative error of at most 0.0003.
Values sent between devices are 32-bit elements; how exact they have to be, the bound alone decides.
A program may use at most 64 MiB of HBM per device.

v0:
```python
import jax
import jax.numpy as jnp
from jax import lax
from jax.sharding import PartitionSpec as P

PATCH = 256


def extended(block, sides, width):
    for axis, dim in sides:
        count = lax.axis_size(axis)
        forward = [(i, i + 1) for i in range(count - 1)]
        backward = [(target, source) for source, target in forward]
        low = lax.ppermute(
            lax.slice_in_dim(block, block.shape[dim] - width, None, axis=dim), axis, forward
        )
        high = lax.ppermute(lax.slice_in_dim(block, 0, width, axis=dim), axis, backward)
        block = jnp.concatenate([low, block, high], axis=dim)
    return block


def advance(padded, coef_y, coef_x, coef_k):
    center = padded[..., 2:-2, :]
    above = padded[..., 3:-1, :]
    below = padded[..., 1:-3, :]
    grad_y = (-padded[..., 4:, :] + 8.0 * above - 8.0 * below + padded[..., :-4, :]) / 12.0
    lap_y = above - 2.0 * center + below
    right_one = jnp.roll(center, -1, axis=-1)
    left_one = jnp.roll(center, 1, axis=-1)
    grad_x = (
        -jnp.roll(center, -2, axis=-1)
        + 8.0 * right_one
        - 8.0 * left_one
        + jnp.roll(center, 2, axis=-1)
    ) / 12.0
    lap_x = right_one - 2.0 * center + left_one
    return center - coef_y * grad_y - coef_x * grad_x + coef_k * (lap_y + lap_x)


def analyze(members, cells, observed, variance):
    ensemble_size = members.shape[0]
    highest = lax.Precision.HIGHEST
    center = jnp.mean(members, axis=0)
    spread = members - center[None, :]
    obs_spread = jnp.take(spread, cells, axis=1)
    innovation = observed - jnp.take(center, cells)
    weighted = obs_spread / variance[None, :]
    gram = jnp.dot(weighted, obs_spread.T, precision=highest, preferred_element_type=jnp.float32)
    system = gram + (ensemble_size - 1.0) * jnp.eye(ensemble_size, dtype=jnp.float32)
    factor = jnp.linalg.cholesky(system)
    pulled = jnp.dot(weighted, innovation, precision=highest, preferred_element_type=jnp.float32)
    right_side = jnp.concatenate([pulled[:, None], gram], axis=1)
    solved = jax.scipy.linalg.cho_solve((factor, True), right_side)
    gain_mean = solved[:, 0]
    mixing = solved[:, 1:]
    transform = jnp.eye(ensemble_size, dtype=jnp.float32) - 0.5 * mixing + gain_mean[None, :]
    return center[None, :] + jnp.dot(
        transform, spread, precision=highest, preferred_element_type=jnp.float32
    )


def on_device(prior_ensemble_fields, vel_y, vel_x, diffus, assign, obs_cell, obs_value, obs_var):
    local_members, tile_rows, width_cells = prior_ensemble_fields.shape
    columns = tile_rows * width_cells
    groups = lax.axis_size("mem")
    group_columns = columns // groups
    patches_here = group_columns // PATCH
    ensemble = prior_ensemble_fields
    stacked = jnp.concatenate([ensemble, vel_y[None], vel_x[None], diffus[None]], axis=0)
    widened = extended(stacked, (("tile", 1),), 4)
    field_rows = widened[:local_members]
    near_y = widened[local_members, 2:-2]
    near_x = widened[local_members + 1, 2:-2]
    near_k = widened[local_members + 2, 2:-2]
    middle = advance(field_rows, near_y, near_x, near_k)
    first_row = lax.axis_index("tile") * tile_rows - 2
    global_rows = first_row + jnp.arange(tile_rows + 4, dtype=jnp.int32)
    inside = (global_rows >= 0) & (global_rows < tile_rows * lax.axis_size("tile"))
    middle = jnp.where(inside[None, :, None], middle, 0.0)
    ensemble = advance(middle, vel_y, vel_x, diffus)
    order = assign[0]
    permuted = jnp.take(ensemble.reshape(local_members, columns), order, axis=1)
    blocks = permuted.reshape(local_members, groups, group_columns)
    gathered = lax.all_to_all(blocks, "mem", split_axis=1, concat_axis=0, tiled=True)
    gathered = gathered.reshape(local_members * groups, patches_here, PATCH)
    updated = jax.vmap(analyze, in_axes=(1, 0, 0, 0), out_axes=1)(
        gathered, obs_cell, obs_value, obs_var
    )
    outgoing = updated.reshape(local_members * groups, 1, group_columns)
    returned = lax.all_to_all(outgoing, "mem", split_axis=0, concat_axis=1, tiled=True)
    returned = returned.reshape(local_members, columns)
    positions = jnp.argsort(order)
    analysed = jnp.take(returned, positions, axis=1).reshape(local_members, tile_rows, width_cells)
    padded = extended(analysed, (("tile", 1),), 2)
    return advance(padded, vel_y, vel_x, diffus)


def solution(mesh):
    return jax.shard_map(
        on_device,
        mesh=mesh,
        in_specs=(
            P("mem", "tile", None),
            P("tile", None),
            P("tile", None),
            P("tile", None),
            P("tile", None),
            P(("tile", "mem"), None),
            P(("tile", "mem"), None),
            P(("tile", "mem"), None),
        ),
        out_specs=P("mem", "tile", None),
        check_vma=False,
    )
```

profile of v0, /device:TPU:24, one launch (start us, length us, event | category | flops | bytes accessed | tf_op | source)
XLA Modules:
  0.0 133.3 jit_solution(381985108282282040)
XLA Ops:
  0.0 1.1 pad_maximum_fusion.11
  1.1 3.4 %collective-permute-start = (f32[35,4,512]{2,1,0:T(4,128)S(1)}, f32[35,4,512]{2,1,0:T(4,128)S(1)}, u32[]{:S(2)}, u32[]{:S(2)}) collective-permute-start(f32[35,4,512]{2,1,0:T(4,128)S(1)} %pad_maximum_fusion.11), channel_id=1, source_target_pairs={{0,4},{4,8},{8,12},{12,16},{16,20},{20,24},{24,28},{1,5},{5,9},{9,... | collective-permute-start | bytes 860168 | tf_op jit(solution)/shard_map/ppermute | solution.py:14
  4.5 3.3 %collective-permute-start.1 = (f32[35,4,512]{2,1,0:T(4,128)S(1)}, f32[35,4,512]{2,1,0:T(4,128)S(1)}, u32[]{:S(2)}, u32[]{:S(2)}) collective-permute-start(f32[35,4,512]{2,1,0:T(4,128)S(1)} %pad_maximum_fusion.11), channel_id=1, source_target_pairs={{4,0},{8,4},{12,8},{16,12},{20,16},{24,20},{28,24},{5,1},{9,5},{13... | collective-permute-start | bytes 860168 | tf_op jit(solution)/shard_map/ppermute | solution.py:17
  7.8 0.7 fusion.66
  8.5 0.7 compare_and_fusion.1
  9.3 0.7 fusion.68
  10.0 5.7 %sort.17 = (s32[2048]{0:T(1024)}, s32[2048]{0:T(1024)S(1)}) sort(s32[2048]{0:T(1024)} %bitcast.89, s32[2048]{0:T(1024)S(1)} %iota.82), dimensions={0}, to_apply=%region_3.5 | sort | flops 22528 | bytes 32768 | tf_op jit(solution)/shard_map/jit(argsort)/sort | solution.py:92
  15.8 0.7 broadcast_multiply_fusion
  16.5 2.1 %collective-permute-done.1 = f32[35,4,512]{2,1,0:T(4,128)S(1)} collective-permute-done((f32[35,4,512]{2,1,0:T(4,128)S(1)}, f32[35,4,512]{2,1,0:T(4,128)S(1)}, u32[]{:S(2)}, u32[]{:S(2)}) %collective-permute-start.1) | collective-permute-done | bytes 286752 | tf_op jit(solution)/shard_map/ppermute | solution.py:17
  18.6 1.2 pad_maximum_fusion
  21.1 0.9 fusion.6
  22.6 0.8 fusion.29
  23.7 5.5 %gather_fusion.2 = f32[2048,32]{1,0:T(8,128)S(1)} fusion(f32[32,2048]{0,1:T(8,128)S(1)} %bitcast.66, s32[2048]{0:T(1024)S(1)} %fusion.66), kind=kCustom, calls=%fused_computation.clone | custom fusion | bytes 532480 | tf_op jit(solution)/shard_map/jit(_take)/gather | solution.py:82
  29.6 1.0 copy.82
  30.6 3.6 %all-to-all-start = ((f32[32,4,512]{2,0,1:T(8,128)}), f32[32,4,512]{2,0,1:T(8,128)S(1)}, u32[]{:S(2)}, u32[]{:S(2)}) async-start(f32[32,4,512]{2,0,1:T(8,128)} %copy.82), calls=%async_computation | async-start | bytes 524288 | tf_op jit(solution)/shard_map/all_to_all | solution.py:84
  34.2 5.8 %all-to-all-done = f32[32,4,512]{2,0,1:T(8,128)S(1)} async-done(((f32[32,4,512]{2,0,1:T(8,128)}), f32[32,4,512]{2,0,1:T(8,128)S(1)}, u32[]{:S(2)}, u32[]{:S(2)}) %all-to-all-start) | async-done | bytes 262176 | tf_op jit(solution)/shard_map/all_to_all | solution.py:84
  40.5 9.1 %gather_fusion.1 = f32[1024]{0:T(1024)S(1)} fusion(f32[2,256]{1,0:T(2,128)S(1)} %div.32, s32[1024]{0:T(1024)S(1)} %bitcast.64), kind=kCustom, calls=%fused_computation.3 | custom fusion | bytes 16384 | tf_op jit(solution)/shard_map/vmap(jit(_take))/gather | solution.py:46
  49.6 6.8 %gather_fusion = f32[1024,128]{1,0:T(8,128)S(1)} fusion(f32[2,128,256]{1,2,0:T(8,128)S(1)} %subtract_bitcast_fusion, s32[1024]{0:T(1024)S(1)} %bitcast.65), kind=kCustom, calls=%fused_computation.2 | custom fusion | bytes 1056768 | tf_op jit(solution)/shard_map/vmap(jit(_take))/gather | solution.py:45
  56.5 1.8 %fusion.14 = f32[2,128,128]{1,2,0:T(8,128)S(1)} fusion(f32[2,512,128]{2,1,0:T(8,128)S(1)} %bitcast.73, f32[2,512]{1,0:T(2,128)S(1)} %copy-done.6, pred[2,512]{1,0:T(4,128)(4,1)S(1)} %get-tuple-element.9), kind=kOutput, calls=%fused_computation.38 | convolution fusion | flops 201719808 | bytes 660480 | tf_op jit(solution)/shard_map/vmap()/dot_general | solution.py:48
  58.5 23.5 %custom-call.11 = f32[2,128,128]{2,1,0:T(8,128)S(1)} custom-call(f32[2,128,128]{2,1,0:T(8,128)S(1)} %fusion.54), custom_call_target="Cholesky" | custom-call | tf_op jit(solution)/shard_map/vmap(jit(cholesky))/cholesky | solution.py:50
  82.2 19.7 %custom-call.12 = f32[2,1,128,128]{2,3,1,0:T(8,128)S(1)} custom-call(f32[2,1,128,128]{3,2,1,0:T(8,128)S(1)} %select_bitcast_fusion), custom_call_target="InvertDiagBlocksLowerTriangular" | custom-call | tf_op jit(solution)/shard_map/vmap(jit(_cho_solve))/triangular_solve | solution.py:53
  101.9 0.6 convolution_bitcast_fusion
  103.4 0.5 fusion
  104.0 0.8 copy.91
  104.9 3.4 %all-to-all-start.1 = ((f32[128,1,512]{2,1,0:T(1,128)}), f32[128,1,512]{2,1,0:T(1,128)S(1)}, u32[]{:S(2)}, u32[]{:S(2)}) async-start(f32[128,1,512]{2,1,0:T(1,128)} %copy.91), calls=%async_computation.1 | async-start | bytes 524288 | tf_op jit(solution)/shard_map/all_to_all | solution.py:90
  108.3 6.0 %all-to-all-done.1 = f32[128,1,512]{2,1,0:T(1,128)S(1)} async-done(((f32[128,1,512]{2,1,0:T(1,128)}), f32[128,1,512]{2,1,0:T(1,128)S(1)}, u32[]{:S(2)}, u32[]{:S(2)}) %all-to-all-start.1) | async-done | bytes 262176 | tf_op jit(solution)/shard_map/all_to_all | solution.py:90
  114.6 5.5 %gather_fusion.3 = f32[2048,32]{1,0:T(8,128)S(1)} fusion(f32[32,2048]{0,1:T(8,128)S(1)} %bitcast.67, s32[2048]{0:T(1024)S(1)} %fusion.67), kind=kCustom, calls=%fused_computation.1.clone | custom fusion | bytes 532480 | tf_op jit(solution)/shard_map/jit(_take)/gather | solution.py:93
  121.4 2.4 %collective-permute-start.2 = (f32[32,2,512]{2,1,0:T(2,128)S(1)}, f32[32,2,512]{2,1,0:T(2,128)S(1)}, u32[]{:S(2)}, u32[]{:S(2)}) collective-permute-start(f32[32,2,512]{2,1,0:T(2,128)S(1)} %get-tuple-element.38), channel_id=1, source_target_pairs={{4,0},{8,4},{12,8},{16,12},{20,16},{24,20},{28,24},{5,1},{9,5},{13... | collective-permute-start | bytes 393224 | tf_op jit(solution)/shard_map/ppermute | solution.py:17
  123.8 3.5 %collective-permute-start.3 = (f32[32,2,512]{2,1,0:T(2,128)S(1)}, f32[32,2,512]{2,1,0:T(2,128)S(1)}, u32[]{:S(2)}, u32[]{:S(2)}) collective-permute-start(f32[32,2,512]{2,1,0:T(2,128)S(1)} %get-tuple-element.37), channel_id=1, source_target_pairs={{0,4},{4,8},{8,12},{12,16},{16,20},{20,24},{24,28},{1,5},{5,9},{9,... | collective-permute-start | bytes 393224 | tf_op jit(solution)/shard_map/ppermute | solution.py:14
  127.3 0.9 collective-permute-done.2
  128.2 3.3 %collective-permute-done.3 = f32[32,2,512]{2,1,0:T(2,128)S(1)} collective-permute-done((f32[32,2,512]{2,1,0:T(2,128)S(1)}, f32[32,2,512]{2,1,0:T(2,128)S(1)}, u32[]{:S(2)}, u32[]{:S(2)}) %collective-permute-start.3) | collective-permute-done | bytes 131104 | tf_op jit(solution)/shard_map/ppermute | solution.py:14
  131.5 1.7 %fusion.25 = f32[32,4,512]{2,1,0:T(4,128)} fusion(f32[32,4,512]{2,1,0:T(4,128)S(1)} %copy.97, f32[32,2,512]{2,1,0:T(2,128)S(1)} %collective-permute-done.2, f32[32,2,512]{2,1,0:T(2,128)S(1)} %collective-permute-done.3, f32[32,4,2]{2,1,0:T(4,128)S(1)} %get-tuple-element.34, f32[32,4,510]{2,1,0:T(4,128)S(1)} %get-tuple-element.36, ...), kind=kLoop, calls=%fused_computation.51 | loop fusion | flops 2097152 | bytes 1859584 | tf_op jit(solution)/shard_map/add | solution.py:37
  (63 shorter events, 6.2 us)
Async XLA Ops:
  1.1 15.4 %collective-permute-start = (f32[35,4,512]{2,1,0:T(4,128)S(1)}, f32[35,4,512]{2,1,0:T(4,128)S(1)}, u32[]{:S(2)}, u32[]{:S(2)}) collective-permute-start(f32[35,4,512]{2,1,0:T(4,128)S(1)} %pad_maximum_fusion.11), channel_id=1, source_target_pairs={{0,4},{4,8},{8,12},{12,16},{16,20},{20,24},{24,28},{1,5},{5,9},{9,... | collective-permute-start | bytes 860168 | tf_op jit(solution)/shard_map/ppermute | solution.py:14
  4.5 14.1 %collective-permute-start.1 = (f32[35,4,512]{2,1,0:T(4,128)S(1)}, f32[35,4,512]{2,1,0:T(4,128)S(1)}, u32[]{:S(2)}, u32[]{:S(2)}) collective-permute-start(f32[35,4,512]{2,1,0:T(4,128)S(1)} %pad_maximum_fusion.11), channel_id=1, source_target_pairs={{4,0},{8,4},{12,8},{16,12},{20,16},{24,20},{28,24},{5,1},{9,5},{13... | collective-permute-start | bytes 860168 | tf_op jit(solution)/shard_map/ppermute | solution.py:17
  20.1 1.0 copy-start
  20.1 0.9 copy-start.1
  20.1 0.9 copy-start.2
  20.1 0.9 copy-start.3
  30.6 9.4 %all-to-all-start = ((f32[32,4,512]{2,0,1:T(8,128)}), f32[32,4,512]{2,0,1:T(8,128)S(1)}, u32[]{:S(2)}, u32[]{:S(2)}) async-start(f32[32,4,512]{2,0,1:T(8,128)} %copy.82), calls=%async_computation | async-start | bytes 524288 | tf_op jit(solution)/shard_map/all_to_all | solution.py:84
  49.6 6.8 %copy-start.4 = (s32[2,512]{1,0:T(2,128)S(1)}, s32[2,512]{1,0:T(2,128)}, u32[]{:S(2)}) copy-start(s32[2,512]{1,0:T(2,128)} %param.15) | copy-start | bytes 12292
  49.6 6.8 %copy-start.5 = (f32[2,512]{1,0:T(2,128)S(1)}, f32[2,512]{1,0:T(2,128)}, u32[]{:S(2)}) copy-start(f32[2,512]{1,0:T(2,128)} %param.16) | copy-start | bytes 12292
  49.6 6.9 %copy-start.6 = (f32[2,512]{1,0:T(2,128)S(1)}, f32[2,512]{1,0:T(2,128)}, u32[]{:S(2)}) copy-start(f32[2,512]{1,0:T(2,128)} %param.17) | copy-start | bytes 12292
  104.9 9.4 %all-to-all-start.1 = ((f32[128,1,512]{2,1,0:T(1,128)}), f32[128,1,512]{2,1,0:T(1,128)S(1)}, u32[]{:S(2)}, u32[]{:S(2)}) async-start(f32[128,1,512]{2,1,0:T(1,128)} %copy.91), calls=%async_computation.1 | async-start | bytes 524288 | tf_op jit(solution)/shard_map/all_to_all | solution.py:90
  121.4 6.9 %collective-permute-start.2 = (f32[32,2,512]{2,1,0:T(2,128)S(1)}, f32[32,2,512]{2,1,0:T(2,128)S(1)}, u32[]{:S(2)}, u32[]{:S(2)}) collective-permute-start(f32[32,2,512]{2,1,0:T(2,128)S(1)} %get-tuple-element.38), channel_id=1, source_target_pairs={{4,0},{8,4},{12,8},{16,12},{20,16},{24,20},{28,24},{5,1},{9,5},{13... | collective-permute-start | bytes 393224 | tf_op jit(solution)/shard_map/ppermute | solution.py:17
  123.8 7.8 %collective-permute-start.3 = (f32[32,2,512]{2,1,0:T(2,128)S(1)}, f32[32,2,512]{2,1,0:T(2,128)S(1)}, u32[]{:S(2)}, u32[]{:S(2)}) collective-permute-start(f32[32,2,512]{2,1,0:T(2,128)S(1)} %get-tuple-element.37), channel_id=1, source_target_pairs={{0,4},{4,8},{8,12},{12,16},{16,20},{20,24},{24,28},{1,5},{5,9},{9,... | collective-permute-start | bytes 393224 | tf_op jit(solution)/shard_map/ppermute | solution.py:14
where the time goes:
time: 134 us; the launch traced here: 133 us
  other arithmetic  58.6 us (44%)
  local copies, waits for them, and re-layouts  32.9 us (25%)
  starting transfers between devices  19.6 us (15%)
  waiting for transfers between devices  18 us (13%)
  matrix products  3.7 us (3%)
    another operation x3, other arithmetic, analyze(): factor = jnp.linalg.cholesky(system)  23.6 us
    another operation x3, other arithmetic, analyze(): solved = jax.scipy.linalg.cho_solve((factor, True), right_side)  19.8 us
    gather x2, local copies, waits for them, and re-layouts, analyze(): innovation = observed - jnp.take(center, cells)  9.12 us
    ppermute x2, starting transfers between devices, extended(): lax.ppermute(lax.slice_in_dim(block, block.shape[dim] - width, None, axis...  6.86 us
    gather x1, local copies, waits for them, and re-layouts, analyze(): obs_spread = jnp.take(spread, cells, axis=1)  6.79 us
    all_to_all x1, waiting for transfers between devices, on_device(): lax.all_to_all(outgoing, 'mem', split_axis=0, concat_axis=1, tiled=True)  5.96 us
    all_to_all x1, waiting for transfers between devices, on_device(): lax.all_to_all(blocks, 'mem', split_axis=1, concat_axis=0, tiled=True)  5.78 us
    sort x1, other arithmetic, on_device(): positions = jnp.argsort(order)  5.74 us
  transfers between devices with their start and end apart: 6, of which 5 were waited for; matrix products, arithmetic and copies ran while one was open for 7% of the time, Pallas kernels for 0%

commit v1 on v0

--- a/solution.py
+++ b/solution.py
@@ -81,7 +81,10 @@
     order = assign[0]
     permuted = jnp.take(ensemble.reshape(local_members, columns), order, axis=1)
     blocks = permuted.reshape(local_members, groups, group_columns)
-    gathered = lax.all_to_all(blocks, "mem", split_axis=1, concat_axis=0, tiled=True)
+    gathered = jnp.concatenate(
+        lax.all_to_all(jnp.stack(jnp.split(blocks, lax.axis_size("mem"), axis=1)), "mem", 0, 0),
+        axis=0,
+    )
     gathered = gathered.reshape(local_members * groups, patches_here, PATCH)
     updated = jax.vmap(analyze, in_axes=(1, 0, 0, 0), out_axes=1)(
         gathered, obs_cell, obs_value, obs_var

time: 134 us -> 134 us (level)
  no operation moved by 1% of the time
where the time goes in v1:
time: 134 us; the launch traced here: 133 us
  other arithmetic  59.4 us (44%)
  local copies, waits for them, and re-layouts  32.4 us (24%)
  starting transfers between devices  19.6 us (15%)
  waiting for transfers between devices  18 us (13%)
  matrix products  3.69 us (3%)
    another operation x3, other arithmetic, analyze(): factor = jnp.linalg.cholesky(system)  23.6 us
    another operation x3, other arithmetic, analyze(): solved = jax.scipy.linalg.cho_solve((factor, True), right_side)  19.8 us
    gather x2, local copies, waits for them, and re-layouts, analyze(): innovation = observed - jnp.take(center, cells)  9.12 us
    ppermute x2, starting transfers between devices, extended(): lax.ppermute(lax.slice_in_dim(block, block.shape[dim] - width, None, axis...  6.85 us
    gather x1, local copies, waits for them, and re-layouts, analyze(): obs_spread = jnp.take(spread, cells, axis=1)  6.79 us
    all_to_all x1, waiting for transfers between devices, on_device(): lax.all_to_all(outgoing, 'mem', split_axis=0, concat_axis=1, tiled=True)  5.96 us
    all_to_all x1, waiting for transfers between devices, on_device(): lax.all_to_all(jnp.stack(jnp.split(blocks, lax.axis_size('mem'), axis=1))...  5.78 us
    sort x1, other arithmetic, on_device(): positions = jnp.argsort(order)  5.74 us
  transfers between devices with their start and end apart: 6, of which 5 were waited for; matrix products, arithmetic and copies ran while one was open for 7% of the time, Pallas kernels for 0%

profile of v1, /device:TPU:24, one launch (start us, length us, event | category | flops | bytes accessed | tf_op | source)
XLA Modules:
  0.0 133.5 jit_solution(9395561147611919042)
XLA Ops:
  0.0 1.1 pad_maximum_fusion.11
  1.1 3.4 %collective-permute-start = (f32[35,4,512]{2,1,0:T(4,128)S(1)}, f32[35,4,512]{2,1,0:T(4,128)S(1)}, u32[]{:S(2)}, u32[]{:S(2)}) collective-permute-start(f32[35,4,512]{2,1,0:T(4,128)S(1)} %pad_maximum_fusion.11), channel_id=1, source_target_pairs={{0,4},{4,8},{8,12},{12,16},{16,20},{20,24},{24,28},{1,5},{5,9},{9,... | collective-permute-start | bytes 860168 | tf_op jit(solution)/shard_map/ppermute | solution.py:14
  4.5 3.3 %collective-permute-start.1 = (f32[35,4,512]{2,1,0:T(4,128)S(1)}, f32[35,4,512]{2,1,0:T(4,128)S(1)}, u32[]{:S(2)}, u32[]{:S(2)}) collective-permute-start(f32[35,4,512]{2,1,0:T(4,128)S(1)} %pad_maximum_fusion.11), channel_id=1, source_target_pairs={{4,0},{8,4},{12,8},{16,12},{20,16},{24,20},{28,24},{5,1},{9,5},{13... | collective-permute-start | bytes 860168 | tf_op jit(solution)/shard_map/ppermute | solution.py:17
  7.8 0.7 fusion.66
  8.5 0.7 compare_and_fusion.1
  9.3 0.7 fusion.68
  10.0 5.7 %sort.17 = (s32[2048]{0:T(1024)}, s32[2048]{0:T(1024)S(1)}) sort(s32[2048]{0:T(1024)} %bitcast.93, s32[2048]{0:T(1024)S(1)} %iota.82), dimensions={0}, to_apply=%region_3.5 | sort | flops 22528 | bytes 32768 | tf_op jit(solution)/shard_map/jit(argsort)/sort | solution.py:95
  15.8 0.7 broadcast_multiply_fusion
  16.5 2.1 %collective-permute-done.1 = f32[35,4,512]{2,1,0:T(4,128)S(1)} collective-permute-done((f32[35,4,512]{2,1,0:T(4,128)S(1)}, f32[35,4,512]{2,1,0:T(4,128)S(1)}, u32[]{:S(2)}, u32[]{:S(2)}) %collective-permute-start.1) | collective-permute-done | bytes 286752 | tf_op jit(solution)/shard_map/ppermute | solution.py:17
  18.6 1.2 pad_maximum_fusion
  21.1 0.9 fusion.6
  22.6 0.8 fusion.29
  23.7 5.5 %gather_fusion.2 = f32[2048,32]{1,0:T(8,128)S(1)} fusion(f32[32,2048]{0,1:T(8,128)S(1)} %bitcast.67, s32[2048]{0:T(1024)S(1)} %fusion.66), kind=kCustom, calls=%fused_computation.clone | custom fusion | bytes 532480 | tf_op jit(solution)/shard_map/jit(_take)/gather | solution.py:82
  30.1 0.7 pad_maximum_fusion.16
  30.8 3.6 %all-to-all-start = ((f32[4,32,1,512]{3,1,2,0:T(8,128)}), f32[4,32,1,512]{3,1,2,0:T(8,128)S(1)}, u32[]{:S(2)}, u32[]{:S(2)}) async-start(f32[4,32,1,512]{3,1,2,0:T(8,128)} %pad_maximum_fusion.16), calls=%async_computation | async-start | bytes 524288 | tf_op jit(solution)/shard_map/all_to_all | solution.py:85
  34.4 5.8 %all-to-all-done = f32[4,32,1,512]{3,1,2,0:T(8,128)S(1)} async-done(((f32[4,32,1,512]{3,1,2,0:T(8,128)}), f32[4,32,1,512]{3,1,2,0:T(8,128)S(1)}, u32[]{:S(2)}, u32[]{:S(2)}) %all-to-all-start) | async-done | bytes 262176 | tf_op jit(solution)/shard_map/all_to_all | solution.py:85
  40.7 9.1 %gather_fusion.1 = f32[1024]{0:T(1024)S(1)} fusion(f32[2,256]{1,0:T(2,128)S(1)} %div.32, s32[1024]{0:T(1024)S(1)} %bitcast.65), kind=kCustom, calls=%fused_computation.3 | custom fusion | bytes 16384 | tf_op jit(solution)/shard_map/vmap(jit(_take))/gather | solution.py:46
  49.9 6.8 %gather_fusion = f32[1024,128]{1,0:T(8,128)S(1)} fusion(f32[2,128,256]{1,2,0:T(8,128)S(1)} %subtract_bitcast_fusion, s32[1024]{0:T(1024)S(1)} %bitcast.66), kind=kCustom, calls=%fused_computation.2 | custom fusion | bytes 1056768 | tf_op jit(solution)/shard_map/vmap(jit(_take))/gather | solution.py:45
  56.7 1.8 %fusion.14 = f32[2,128,128]{1,2,0:T(8,128)S(1)} fusion(f32[2,512,128]{2,1,0:T(8,128)S(1)} %bitcast.73, f32[2,512]{1,0:T(2,128)S(1)} %copy-done.6, pred[2,512]{1,0:T(4,128)(4,1)S(1)} %get-tuple-element.9), kind=kOutput, calls=%fused_computation.38 | convolution fusion | flops 201719808 | bytes 660480 | tf_op jit(solution)/shard_map/vmap()/dot_general | solution.py:48
  58.7 23.5 %custom-call.11 = f32[2,128,128]{2,1,0:T(8,128)S(1)} custom-call(f32[2,128,128]{2,1,0:T(8,128)S(1)} %fusion.54), custom_call_target="Cholesky" | custom-call | tf_op jit(solution)/shard_map/vmap(jit(cholesky))/cholesky | solution.py:50
  82.4 19.7 %custom-call.12 = f32[2,1,128,128]{2,3,1,0:T(8,128)S(1)} custom-call(f32[2,1,128,128]{3,2,1,0:T(8,128)S(1)} %select_bitcast_fusion), custom_call_target="InvertDiagBlocksLowerTriangular" | custom-call | tf_op jit(solution)/shard_map/vmap(jit(_cho_solve))/triangular_solve | solution.py:53
  102.1 0.6 convolution_bitcast_fusion
  103.6 0.5 fusion
  104.2 0.8 copy.100
  105.1 3.4 %all-to-all-start.1 = ((f32[128,1,512]{2,1,0:T(1,128)}), f32[128,1,512]{2,1,0:T(1,128)S(1)}, u32[]{:S(2)}, u32[]{:S(2)}) async-start(f32[128,1,512]{2,1,0:T(1,128)} %copy.100), calls=%async_computation.1 | async-start | bytes 524288 | tf_op jit(solution)/shard_map/all_to_all | solution.py:93
  108.5 6.0 %all-to-all-done.1 = f32[128,1,512]{2,1,0:T(1,128)S(1)} async-done(((f32[128,1,512]{2,1,0:T(1,128)}), f32[128,1,512]{2,1,0:T(1,128)S(1)}, u32[]{:S(2)}, u32[]{:S(2)}) %all-to-all-start.1) | async-done | bytes 262176 | tf_op jit(solution)/shard_map/all_to_all | solution.py:93
  114.8 5.5 %gather_fusion.3 = f32[2048,32]{1,0:T(8,128)S(1)} fusion(f32[32,2048]{0,1:T(8,128)S(1)} %bitcast.68, s32[2048]{0:T(1024)S(1)} %fusion.67), kind=kCustom, calls=%fused_computation.1.clone | custom fusion | bytes 532480 | tf_op jit(solution)/shard_map/jit(_take)/gather | solution.py:96
  121.6 2.4 %collective-permute-start.2 = (f32[32,2,512]{2,1,0:T(2,128)S(1)}, f32[32,2,512]{2,1,0:T(2,128)S(1)}, u32[]{:S(2)}, u32[]{:S(2)}) collective-permute-start(f32[32,2,512]{2,1,0:T(2,128)S(1)} %get-tuple-element.42), channel_id=1, source_target_pairs={{4,0},{8,4},{12,8},{16,12},{20,16},{24,20},{28,24},{5,1},{9,5},{13... | collective-permute-start | bytes 393224 | tf_op jit(solution)/shard_map/ppermute | solution.py:17
  124.0 3.5 %collective-permute-start.3 = (f32[32,2,512]{2,1,0:T(2,128)S(1)}, f32[32,2,512]{2,1,0:T(2,128)S(1)}, u32[]{:S(2)}, u32[]{:S(2)}) collective-permute-start(f32[32,2,512]{2,1,0:T(2,128)S(1)} %get-tuple-element.41), channel_id=1, source_target_pairs={{0,4},{4,8},{8,12},{12,16},{16,20},{20,24},{24,28},{1,5},{5,9},{9,... | collective-permute-start | bytes 393224 | tf_op jit(solution)/shard_map/ppermute | solution.py:14
  127.6 0.9 collective-permute-done.2
  128.5 3.3 %collective-permute-done.3 = f32[32,2,512]{2,1,0:T(2,128)S(1)} collective-permute-done((f32[32,2,512]{2,1,0:T(2,128)S(1)}, f32[32,2,512]{2,1,0:T(2,128)S(1)}, u32[]{:S(2)}, u32[]{:S(2)}) %collective-permute-start.3) | collective-permute-done | bytes 131104 | tf_op jit(solution)/shard_map/ppermute | solution.py:14
  131.8 1.7 %fusion.25 = f32[32,4,512]{2,1,0:T(4,128)} fusion(f32[32,4,512]{2,1,0:T(4,128)S(1)} %copy.106, f32[32,2,512]{2,1,0:T(2,128)S(1)} %collective-permute-done.2, f32[32,2,512]{2,1,0:T(2,128)S(1)} %collective-permute-done.3, f32[32,4,2]{2,1,0:T(4,128)S(1)} %get-tuple-element.38, f32[32,4,510]{2,1,0:T(4,128)S(1)} %get-tuple-element.40, ...), kind=kLoop, calls=%fused_computation.51 | loop fusion | flops 2097152 | bytes 1859584 | tf_op jit(solution)/shard_map/add | solution.py:37
  (68 shorter events, 6.7 us)
Async XLA Ops:
  1.1 15.4 %collective-permute-start = (f32[35,4,512]{2,1,0:T(4,128)S(1)}, f32[35,4,512]{2,1,0:T(4,128)S(1)}, u32[]{:S(2)}, u32[]{:S(2)}) collective-permute-start(f32[35,4,512]{2,1,0:T(4,128)S(1)} %pad_maximum_fusion.11), channel_id=1, source_target_pairs={{0,4},{4,8},{8,12},{12,16},{16,20},{20,24},{24,28},{1,5},{5,9},{9,... | collective-permute-start | bytes 860168 | tf_op jit(solution)/shard_map/ppermute | solution.py:14
  4.5 14.1 %collective-permute-start.1 = (f32[35,4,512]{2,1,0:T(4,128)S(1)}, f32[35,4,512]{2,1,0:T(4,128)S(1)}, u32[]{:S(2)}, u32[]{:S(2)}) collective-permute-start(f32[35,4,512]{2,1,0:T(4,128)S(1)} %pad_maximum_fusion.11), channel_id=1, source_target_pairs={{4,0},{8,4},{12,8},{16,12},{20,16},{24,20},{28,24},{5,1},{9,5},{13... | collective-permute-start | bytes 860168 | tf_op jit(solution)/shard_map/ppermute | solution.py:17
  20.1 1.0 copy-start
  20.1 0.9 copy-start.1
  20.1 0.9 copy-start.2
  20.1 0.9 copy-start.3
  30.8 9.4 %all-to-all-start = ((f32[4,32,1,512]{3,1,2,0:T(8,128)}), f32[4,32,1,512]{3,1,2,0:T(8,128)S(1)}, u32[]{:S(2)}, u32[]{:S(2)}) async-start(f32[4,32,1,512]{3,1,2,0:T(8,128)} %pad_maximum_fusion.16), calls=%async_computation | async-start | bytes 524288 | tf_op jit(solution)/shard_map/all_to_all | solution.py:85
  49.8 6.8 %copy-start.4 = (s32[2,512]{1,0:T(2,128)S(1)}, s32[2,512]{1,0:T(2,128)}, u32[]{:S(2)}) copy-start(s32[2,512]{1,0:T(2,128)} %param.15) | copy-start | bytes 12292
  49.8 6.8 %copy-start.5 = (f32[2,512]{1,0:T(2,128)S(1)}, f32[2,512]{1,0:T(2,128)}, u32[]{:S(2)}) copy-start(f32[2,512]{1,0:T(2,128)} %param.16) | copy-start | bytes 12292
  49.9 6.9 %copy-start.6 = (f32[2,512]{1,0:T(2,128)S(1)}, f32[2,512]{1,0:T(2,128)}, u32[]{:S(2)}) copy-start(f32[2,512]{1,0:T(2,128)} %param.17) | copy-start | bytes 12292
  105.1 9.4 %all-to-all-start.1 = ((f32[128,1,512]{2,1,0:T(1,128)}), f32[128,1,512]{2,1,0:T(1,128)S(1)}, u32[]{:S(2)}, u32[]{:S(2)}) async-start(f32[128,1,512]{2,1,0:T(1,128)} %copy.100), calls=%async_computation.1 | async-start | bytes 524288 | tf_op jit(solution)/shard_map/all_to_all | solution.py:93
  121.6 6.9 %collective-permute-start.2 = (f32[32,2,512]{2,1,0:T(2,128)S(1)}, f32[32,2,512]{2,1,0:T(2,128)S(1)}, u32[]{:S(2)}, u32[]{:S(2)}) collective-permute-start(f32[32,2,512]{2,1,0:T(2,128)S(1)} %get-tuple-element.42), channel_id=1, source_target_pairs={{4,0},{8,4},{12,8},{16,12},{20,16},{24,20},{28,24},{5,1},{9,5},{13... | collective-permute-start | bytes 393224 | tf_op jit(solution)/shard_map/ppermute | solution.py:17
  124.0 7.8 %collective-permute-start.3 = (f32[32,2,512]{2,1,0:T(2,128)S(1)}, f32[32,2,512]{2,1,0:T(2,128)S(1)}, u32[]{:S(2)}, u32[]{:S(2)}) collective-permute-start(f32[32,2,512]{2,1,0:T(2,128)S(1)} %get-tuple-element.41), channel_id=1, source_target_pairs={{0,4},{4,8},{8,12},{12,16},{16,20},{20,24},{24,28},{1,5},{5,9},{9,... | collective-permute-start | bytes 393224 | tf_op jit(solution)/shard_map/ppermute | solution.py:14
